TPU v7x, 32 devices: a whole 2x2x4 slice. The times are simulated.
32 devices in a mesh: dp: 8 (over y, x, core), head: 4 (over z).
Axes of the slice: x: 2, y: 2, z: 4, core: 2. Of those that a mesh axis runs over, the one named last changes fastest.
Arguments:
- tokens: bfloat16 [2048, 2048], P('dp'), may hold values from -6 to 6
- weights: bfloat16 [4, 768, 2048], P('head', 'dp'), may hold values from -0.13479223 to 0.13479223, as said below
- query_gain: float32 [128], replicated, may hold values from 0.25 to 1.75
- key_gain: float32 [128], replicated, may hold values from 0.25 to 1.75
- first_row: int32 [2048], P('dp'), may hold values from 0 to 2047, as said below
- cotangent: bfloat16 [2048, 2048], P('dp', 'head'), may hold values from -6 to 6
Outputs:
- attended: bfloat16 [2048, 2048], P('dp', 'head')
- token_grad: bfloat16 [2048, 2048], P('dp', 'head')
- weight_grad: float32 [4, 768, 2048], P('head', 'dp')
Inputs may be any that keep to these rules, and one draw needn't show every extreme that they name: first_row[i] is the position of the first row of row i's document: documents are runs of consecutive rows, each at most 512 rows long, one of exactly 512 rows, and the last row begins a document of its own. For every even g, weights[g] and weights[g + 1] are equal in their last 256 rows: each key-value head is held by two head devices.
All inputs are finite; a program needn't handle non-finite values.
Results may differ from a plain program's by a relative error of at most 0.017.
Values may be sent and summed in bfloat16 or wider, within the bound.
No kernel may reach another device: no remote copies, remote signals or barrier semaphores. Data moves between devices by JAX's collectives and lax.ppermute only.
A program may use at most 64 MiB of HBM per device.

v0:
```python
import math

import jax
import jax.numpy as jnp
from jax import lax
from jax.sharding import PartitionSpec as P

HD = 128
QH_DEV = 4
COLS = 768
ROWS = 256
SPAN = 2


EPSILON = 1e-06
THETA = 1000000.0
STRETCH = 0.25


def from_behind(x, axis, by):
    devices = lax.axis_size(axis)
    pairs = [(i, i + by) for i in range(devices) if 0 <= i + by < devices]
    return lax.ppermute(x, axis, pairs)


def partner(x, axis, apart):
    return lax.ppermute(x, axis, [(i, i ^ 1 << apart) for i in range(lax.axis_size(axis))])


def rope_tables(position, head_size):
    middle = head_size // 2
    channel = jnp.arange(middle, dtype=jnp.float32)
    frequency = THETA ** (-2.0 * channel / head_size)
    angles = (position.astype(jnp.float32) * STRETCH)[:, None] * frequency[None, :]
    angles = jnp.concatenate([angles, angles], axis=1)
    return (jnp.cos(angles), jnp.sin(angles))


def normalize_rotate(values, scaling, cosine_table, sine_table):
    factor = lax.rsqrt(jnp.mean(values * values, axis=-1, keepdims=True) + EPSILON)
    normed = values * factor * scaling
    middle = normed.shape[-1] // 2
    turned = jnp.concatenate([-normed[..., middle:], normed[..., :middle]], axis=-1)
    return normed * cosine_table + turned * sine_table


def prepare(projected, query_gain, key_gain, cosine_table, sine_table):
    row_count = projected.shape[0]
    queries = projected[:, : QH_DEV * HD].reshape(row_count, QH_DEV, HD)
    queries = normalize_rotate(
        queries, query_gain, cosine_table[:, None, :], sine_table[:, None, :]
    )
    key_part = normalize_rotate(
        projected[:, QH_DEV * HD : (QH_DEV + 1) * HD], key_gain, cosine_table, sine_table
    )
    value_part = projected[:, (QH_DEV + 1) * HD :]
    return (queries, key_part, value_part)


def attend_window(queries, window, upstream, first_rows, query_place, key_place):
    score_scale = 1.0 / math.sqrt(HD)
    key_window = window[:, :HD]
    value_window = window[:, HD:]
    visible = (key_place[None, :] >= first_rows[:, None]) & (
        key_place[None, :] <= query_place[:, None]
    )
    score = (
        jnp.einsum("rhc,kc->rhk", queries, key_window, preferred_element_type=jnp.float32)
        * score_scale
    )
    weight = jnp.where(visible[:, None, :], jnp.exp(score), 0.0)
    denominator = jnp.sum(weight, axis=-1)
    summed = jnp.einsum(
        "rhk,kc->rhc", weight.astype(jnp.bfloat16), value_window, preferred_element_type=jnp.float32
    )
    attended = (summed / denominator[..., None]).astype(jnp.bfloat16)
    probability = weight / denominator[..., None]
    row_delta = jnp.sum(upstream.astype(jnp.float32) * attended.astype(jnp.float32), axis=-1)
    grad_prob = jnp.einsum(
        "rhc,kc->rhk", upstream, value_window, preferred_element_type=jnp.float32
    )
    grad_score = (probability * (grad_prob - row_delta[..., None]) * score_scale).astype(
        jnp.bfloat16
    )
    grad_query = jnp.einsum(
        "rhk,kc->rhc", grad_score, key_window, preferred_element_type=jnp.float32
    )
    grad_key = jnp.einsum("rhk,rhc->kc", grad_score, queries, preferred_element_type=jnp.float32)
    grad_value = jnp.einsum(
        "rhk,rhc->kc",
        probability.astype(jnp.bfloat16),
        upstream,
        preferred_element_type=jnp.float32,
    )
    return (attended, grad_query, jnp.concatenate([grad_key, grad_value], axis=1))


def body(tokens, weights, query_gain, key_gain, first_row, cotangent):
    block_index = lax.axis_index("dp")
    position = block_index * ROWS + jnp.arange(ROWS, dtype=jnp.int32)
    key_place = (block_index - SPAN) * ROWS + jnp.arange((SPAN + 1) * ROWS, dtype=jnp.int32)
    cosine_table, sine_table = rope_tables(position, HD)
    weight_piece = lax.all_gather(weights, "dp", axis=1, tiled=True)
    projected = jnp.einsum("rd,cd->rc", tokens, weight_piece[0], preferred_element_type=jnp.float32)
    prepared, pullback = jax.vjp(
        lambda values: prepare(values, query_gain, key_gain, cosine_table, sine_table), projected
    )
    queries = prepared[0].astype(jnp.bfloat16)
    key_value = jnp.concatenate([prepared[1], prepared[2]], axis=1).astype(jnp.bfloat16)
    earlier = [from_behind(key_value, "dp", distance) for distance in range(SPAN, 0, -1)]
    window = jnp.concatenate(earlier + [key_value], axis=0)
    upstream = cotangent.reshape(ROWS, QH_DEV, HD)
    attended, grad_query, slot_grads = attend_window(
        queries, window, upstream, first_row, position, key_place
    )
    pair_grad = slot_grads[SPAN * ROWS :]
    for distance in range(1, SPAN + 1):
        slot_index = SPAN - distance
        pair_grad = pair_grad + from_behind(
            slot_grads[slot_index * ROWS : (slot_index + 1) * ROWS].astype(jnp.bfloat16),
            "dp",
            -distance,
        ).astype(jnp.float32)
    grad_projected = pullback((grad_query, pair_grad[:, :HD], pair_grad[:, HD:]))[0].astype(
        jnp.bfloat16
    )
    partial_grad = jnp.dot(grad_projected, weight_piece[0], preferred_element_type=jnp.float32)
    token_grad = lax.psum_scatter(
        partial_grad.astype(jnp.bfloat16), "head", scatter_dimension=1, tiled=True
    )
    shard_rows = COLS // lax.axis_size("dp")
    own_grad = lax.psum_scatter(
        jnp.einsum("rc,rd->cd", grad_projected, tokens, preferred_element_type=jnp.float32),
        "dp",
        scatter_dimension=0,
        tiled=True,
    )
    partner_grad = partner(own_grad.astype(jnp.bfloat16), "head", 0).astype(own_grad.dtype)
    global_rows = block_index * shard_rows + jnp.arange(shard_rows, dtype=jnp.int32)
    shared_rows = global_rows >= QH_DEV * HD
    weight_grad = jnp.where(shared_rows[:, None], own_grad + partner_grad, own_grad)
    return (attended.reshape(ROWS, QH_DEV * HD), token_grad, weight_grad[None])


def solution(mesh):
    in_specs = (P("dp", None), P("head", "dp", None), P(), P(), P("dp"), P("dp", "head"))
    out_specs = (P("dp", "head"), P("dp", "head"), P("head", "dp", None))
    return jax.shard_map(body, mesh=mesh, in_specs=in_specs, out_specs=out_specs, check_vma=False)
```

profile of v0, /device:TPU:0, one launch (start us, length us, event | category | flops | bytes accessed | tf_op | source)
XLA Modules:
  0.0 185.5 jit_solution(12164193166599489742)
XLA Ops:
  7.2 0.7 all-gather.2.cloned.1.call-update
  8.0 1.8 copy.66
  9.9 1.6 compare_and_fusion
  11.5 33.3 %all-gather.2.cloned.1.call-done = bf16[1,768,2048]{2,1,0:T(8,128)(2,1)} async-done(((bf16[1,96,2048]{2,1,0:T(8,128)(2,1)}), bf16[1,768,2048]{2,1,0:T(8,128)(2,1)}) %all-gather.2.cloned.1.call-update) | async-done | bytes 3145744 | tf_op jit(solution)/shard_map/all_gather | solution.py:103
  44.8 2.9 %fusion.4 = f32[256,768]{1,0:T(8,128)S(1)} fusion(bf16[256,2048]{1,0:T(8,128)(2,1)S(1)} %copy-done, bf16[1,768,2048]{2,1,0:T(8,128)(2,1)} %all-gather.2.cloned.1.call-done), kind=kOutput, calls=%fused_computation.5 | convolution fusion | flops 805306368 | bytes 4980736 | tf_op jit(solution)/shard_map/rd,cd->rc/dot_general | solution.py:104
  48.1 1.3 fusion.39
  49.4 0.7 pad_maximum_fusion.2
  50.0 2.8 %collective-permute-start.1 = (bf16[256,256]{1,0:T(8,128)(2,1)}, bf16[256,256]{1,0:T(8,128)(2,1)}, u32[]{:S(2)}, u32[]{:S(2)}) collective-permute-start(bf16[256,256]{1,0:T(8,128)(2,1)} %pad_maximum_fusion.2), channel_id=1, source_target_pairs={{0,4},{4,8},{8,12},{12,16},{16,20},{20,24},{24,28},{1,5},{5,9},{9,... | collective-permute-start | bytes 393224 | tf_op jit(solution)/shard_map/ppermute | solution.py:23
  52.8 3.4 %collective-permute-start = (bf16[256,256]{1,0:T(8,128)(2,1)}, bf16[256,256]{1,0:T(8,128)(2,1)}, u32[]{:S(2)}, u32[]{:S(2)}) collective-permute-start(bf16[256,256]{1,0:T(8,128)(2,1)} %pad_maximum_fusion.2), channel_id=1, source_target_pairs={{0,8},{4,12},{8,16},{12,20},{16,24},{20,28},{1,9},{5,13},{9,17},{1... | collective-permute-start | bytes 393224 | tf_op jit(solution)/shard_map/ppermute | solution.py:23
  57.0 1.0 copy.63
  58.6 0.9 collective-permute-done
  59.5 1.0 maximum_maximum_fusion
  60.5 1.0 fusion.10
  61.6 1.4 multiply_reduce_fusion.1
  63.0 1.1 fusion.19
  64.1 1.5 fusion.1
  66.2 0.7 broadcast_multiply_fusion
  67.1 0.7 fusion.50
  67.8 1.3 collective-permute-start.2
  69.1 1.3 collective-permute-start.3
  71.4 7.2 %collective-permute-done.3 = bf16[256,256]{1,0:T(8,128)(2,1)} collective-permute-done((bf16[256,256]{1,0:T(8,128)(2,1)}, bf16[256,256]{1,0:T(8,128)(2,1)}, u32[]{:S(2)}, u32[]{:S(2)}) %collective-permute-start.3) | collective-permute-done | bytes 131104 | tf_op jit(solution)/shard_map/ppermute | solution.py:23
  78.6 1.1 fusion.35
  80.3 0.6 multiply_reduce_fusion.3
  81.1 3.7 %fusion.48 = f32[768,2048]{1,0:T(8,128)} fusion(bf16[256,2048]{1,0:T(8,128)(2,1)S(1)} %copy-done, f32[256,512]{1,0:T(8,128)S(1)} %copy.87, f32[256,128]{1,0:T(8,128)S(1)} %add_add_fusion.1, f32[256,128]{1,0:T(8,128)S(1)} %get-tuple-element.23), kind=kOutput, calls=%fused_computation.82 | convolution fusion | flops 805896192 | bytes 8126464 | tf_op jit(solution)/shard_map/rc,rd->cd/dot_general | solution.py:133
  84.9 3.9 %fusion.6 = bf16[256,2048]{1,0:T(8,128)(2,1)} fusion(bf16[1,768,2048]{2,1,0:T(8,128)(2,1)} %all-gather.2.cloned.1.call-done, f32[256,512]{1,0:T(8,128)S(1)} %copy.87, f32[256,128]{1,0:T(8,128)S(1)} %add_add_fusion.1, f32[256,128]{1,0:T(8,128)S(1)} %get-tuple-element.23), kind=kOutput, calls=%fused_computation.8 | convolution fusion | flops 806420480 | bytes 4980736 | tf_op jit(solution)/shard_map/dot_general | solution.py:127
  88.8 59.1 %reduce-scatter.5.cloned.1.call-done = f32[96,2048]{1,0:T(8,128)} async-done(((f32[768,2048]{1,0:T(8,128)}), f32[96,2048]{1,0:T(8,128)}) %reduce-scatter.5.cloned.1.call-update) | async-done | bytes 786448 | tf_op jit(solution)/shard_map/reduce_scatter | solution.py:132
  147.9 1.2 convert_element_type.61
  149.1 1.6 collective-permute-start.4
  150.6 0.8 copy.75
  151.5 11.0 %collective-permute-done.4 = bf16[96,2048]{1,0:T(8,128)(2,1)S(1)} collective-permute-done((bf16[96,2048]{1,0:T(8,128)(2,1)S(1)}, bf16[96,2048]{1,0:T(8,128)(2,1)S(1)}, u32[]{:S(2)}, u32[]{:S(2)}) %collective-permute-start.4) | collective-permute-done | bytes 393248 | tf_op jit(solution)/shard_map/ppermute | solution.py:27
  162.5 2.2 %fusion.29 = f32[1,96,2048]{2,1,0:T(8,128)} fusion(f32[96,2048]{1,0:T(8,128)} %reduce-scatter.5.cloned.1.call-done, bf16[96,2048]{1,0:T(8,128)(2,1)S(1)} %collective-permute-done.4, pred[96]{0:T(512)(128)(4,1)S(1)} %add_compare_fusion), kind=kLoop, calls=%fused_computation.27 | loop fusion | flops 589824 | bytes 1966176 | tf_op jit(solution)/shard_map/broadcast_in_dim | solution.py:142
  164.7 14.3 %reduce-scatter.3.cloned.1.call-done = bf16[256,512]{1,0:T(8,128)(2,1)} async-done(((bf16[256,2048]{1,0:T(8,128)(2,1)}), bf16[256,512]{1,0:T(8,128)(2,1)}) %reduce-scatter.3.cloned.1.call-update) | async-done | bytes 262160 | tf_op jit(solution)/shard_map/reduce_scatter | solution.py:128
  (53 shorter events, 4.5 us)
Async XLA Ops:
  7.2 37.7 %copy-start = (bf16[256,2048]{1,0:T(8,128)(2,1)S(1)}, bf16[256,2048]{1,0:T(8,128)(2,1)}, u32[]{:S(2)}) copy-start(bf16[256,2048]{1,0:T(8,128)(2,1)} %param.6) | copy-start | bytes 3145732
  7.2 37.6 %all-gather.2.cloned.1.call-start = ((), (), s32[]{:S(2)}) async-start(), calls=%async_computation.2 | async-start | bytes 3538944 | tf_op jit(solution)/shard_map/all_gather | solution.py:103
  7.9 140.0 %reduce-scatter.5.cloned.1.call-start = ((), (), s32[]{:S(2)}) async-start(), calls=%async_computation.4 | async-start | bytes 7077888 | tf_op jit(solution)/shard_map/reduce_scatter | solution.py:132
  9.8 38.1 %copy-start.6 = (f32[128]{0:T(128)S(1)}, f32[128]{0:T(128)}, u32[]{:S(2)}) copy-start(f32[128]{0:T(128)} %param.9) | copy-start | bytes 1540
  47.9 10.4 %copy-start.5 = (f32[128]{0:T(128)S(1)}, f32[128]{0:T(128)}, u32[]{:S(2)}) copy-start(f32[128]{0:T(128)} %param.8) | copy-start | bytes 1540
  50.0 8.5 %collective-permute-start.1 = (bf16[256,256]{1,0:T(8,128)(2,1)}, bf16[256,256]{1,0:T(8,128)(2,1)}, u32[]{:S(2)}, u32[]{:S(2)}) collective-permute-start(bf16[256,256]{1,0:T(8,128)(2,1)} %pad_maximum_fusion.2), channel_id=1, source_target_pairs={{0,4},{4,8},{8,12},{12,16},{16,20},{20,24},{24,28},{1,5},{5,9},{9,... | collective-permute-start | bytes 393224 | tf_op jit(solution)/shard_map/ppermute | solution.py:23
  52.8 6.7 %collective-permute-start = (bf16[256,256]{1,0:T(8,128)(2,1)}, bf16[256,256]{1,0:T(8,128)(2,1)}, u32[]{:S(2)}, u32[]{:S(2)}) collective-permute-start(bf16[256,256]{1,0:T(8,128)(2,1)} %pad_maximum_fusion.2), channel_id=1, source_target_pairs={{0,8},{4,12},{8,16},{12,20},{16,24},{20,28},{1,9},{5,13},{9,17},{1... | collective-permute-start | bytes 393224 | tf_op jit(solution)/shard_map/ppermute | solution.py:23
  58.2 2.3 %copy-start.4 = (pred[256,768]{1,0:T(8,128)(4,1)S(1)}, pred[256,768]{1,0:T(8,128)(4,1)}, u32[]{:S(2)}) copy-start(pred[256,768]{1,0:T(8,128)(4,1)} %compare_and_fusion) | copy-start | bytes 589828
  58.4 3.1 %copy-start.3 = (bf16[256,512]{0,1:T(8,128)(2,1)S(1)}, bf16[256,512]{0,1:T(8,128)(2,1)}, u32[]{:S(2)}) copy-start(bf16[256,512]{0,1:T(8,128)(2,1)} %copy.66) | copy-start | bytes 786436
  64.1 3.0 %copy-start.1 = (f32[768,128]{1,0:T(8,128)}, f32[768,128]{1,0:T(8,128)S(1)}, u32[]{:S(2)}) copy-start(f32[768,128]{1,0:T(8,128)S(1)} %fusion.19) | copy-start | bytes 1179652
  67.8 3.6 %collective-permute-start.2 = (bf16[256,256]{1,0:T(8,128)(2,1)}, bf16[256,256]{1,0:T(8,128)(2,1)}, u32[]{:S(2)}, u32[]{:S(2)}) collective-permute-start(bf16[256,256]{1,0:T(8,128)(2,1)} %get-tuple-element.21), channel_id=1, source_target_pairs={{4,0},{8,4},{12,8},{16,12},{20,16},{24,20},{28,24},{5,1},{9,5},{13... | collective-permute-start | bytes 393224 | tf_op jit(solution)/shard_map/ppermute | solution.py:23
  69.1 9.5 %collective-permute-start.3 = (bf16[256,256]{1,0:T(8,128)(2,1)}, bf16[256,256]{1,0:T(8,128)(2,1)}, u32[]{:S(2)}, u32[]{:S(2)}) collective-permute-start(bf16[256,256]{1,0:T(8,128)(2,1)} %get-tuple-element.22), channel_id=1, source_target_pairs={{8,0},{12,4},{16,8},{20,12},{24,16},{28,20},{9,1},{13,5},{17,9},{2... | collective-permute-start | bytes 393224 | tf_op jit(solution)/shard_map/ppermute | solution.py:23
  84.8 65.8 %copy-start.2 = (bf16[256,4,128]{0,2,1:T(8,128)(2,1)S(1)}, bf16[256,4,128]{0,2,1:T(8,128)(2,1)}, u32[]{:S(2)}) copy-start(bf16[256,4,128]{0,2,1:T(8,128)(2,1)} %get-tuple-element.35) | copy-start | bytes 786436
  84.8 94.1 %reduce-scatter.3.cloned.1.call-start = ((), (), s32[]{:S(2)}) async-start(), calls=%async_computation.3 | async-start | bytes 1310720 | tf_op jit(solution)/shard_map/reduce_scatter | solution.py:128
  149.1 13.5 %collective-permute-start.4 = (bf16[96,2048]{1,0:T(8,128)(2,1)S(1)}, bf16[96,2048]{1,0:T(8,128)(2,1)S(1)}, u32[]{:S(2)}, u32[]{:S(2)}) collective-permute-start(bf16[96,2048]{1,0:T(8,128)(2,1)S(1)} %convert_element_type.61), channel_id=1, source_target_pairs={{0,1},{1,0},{2,3},{3,2},{4,5},{5,4},{6,7},{7,6},{8,9},{9,8},{10,11... | collective-permute-start | bytes 1179656 | tf_op jit(solution)/shard_map/ppermute | solution.py:27
Sparse Core Ops, SparseCore 0:
  9.9 34.8 all-gather.1
  84.9 62.8 reduce-scatter.4
  150.8 28.1 reduce-scatter.2
where the time goes:
time: 186 us
  waiting for transfers between devices  127 us (68%)
  matrix products  16.7 us (9%)
  between operations  14.1 us (8%)
  other arithmetic  11.9 us (6%)
  starting transfers between devices  10.4 us (6%)
  local copies, waits for them, and re-layouts  5.22 us (3%)
    reduce_scatter x1, waiting for transfers between devices, body(): lax.psum_scatter(jnp.einsum('rc,rd->cd', grad_projected, tokens, preferre...  59.1 us
    all_gather x1, waiting for transfers between devices, body(): weight_piece = lax.all_gather(weights, 'dp', axis=1, tiled=True)  33.3 us
    reduce_scatter x1, waiting for transfers between devices, body(): lax.psum_scatter(partial_grad.astype(jnp.bfloat16), 'head', scatter_dimen...  14.3 us
    ppermute x1, waiting for transfers between devices, partner(): lax.ppermute(x, axis, [(i, i ^ 1 << apart) for i in range(lax.axis_size(a...  11 us
    ppermute x4, starting transfers between devices, from_behind(): return lax.ppermute(x, axis, pairs)  8.74 us
    ppermute x4, waiting for transfers between devices, from_behind(): return lax.ppermute(x, axis, pairs)  8.71 us
    dot_general x1, matrix products, body(): jnp.dot(grad_projected, weight_piece[0], preferred_element_type=jnp.float32)  3.86 us
  transfers between devices with their start and end apart: 8, of which 7 were waited for; matrix products, arithmetic and copies ran while one was open for 8% of the time, Pallas kernels for 0%

commit v1 on v0

v1 whole, which is shorter than its diff:
```python
import math

import jax
import jax.numpy as jnp
from jax import lax
from jax.experimental import pallas as pl
from jax.experimental.pallas import tpu as pltpu
from jax.sharding import PartitionSpec as P


MOST = 512
EPSILON = 1e-06
THETA = 1000000.0
STRETCH = 0.25
BF = jnp.bfloat16
F32 = jnp.float32


def swap(x, axis, bits):
    return lax.ppermute(x, axis, [(i, i ^ bits) for i in range(lax.axis_size(axis))])


def rotate(x, axis, by):
    n = lax.axis_size(axis)
    return lax.ppermute(x, axis, [(i, (i + by) % n) for i in range(n)])


def from_behind(x, axis, by):
    n = lax.axis_size(axis)
    return lax.ppermute(x, axis, [(i, i + by) for i in range(n) if 0 <= i + by < n])


def on_core(kernel, outs, args, flops, scratch=(), after=(), mib=16):
    spec = pl.BlockSpec(memory_space=pltpu.VMEM)
    specs = [
        pl.BlockSpec(memory_space=pltpu.SMEM) if a.ndim == 1 else spec for a in args
    ]
    specs += [pl.BlockSpec(memory_space=pl.ANY)] * len(after)

    def run(*refs):
        kernel(*refs[: len(args)], *refs[len(specs) :])

    return pl.pallas_call(
        run,
        out_shape=[jax.ShapeDtypeStruct(s, d) for s, d in outs],
        in_specs=specs,
        out_specs=[spec] * len(outs),
        scratch_shapes=list(scratch),
        compiler_params=pltpu.CompilerParams(vmem_limit_bytes=mib << 20),
        cost_estimate=pl.CostEstimate(flops=flops, bytes_accessed=1 << 20, transcendentals=0),
    )(*args, *after)


def later(x, after):
    return lax.optimization_barrier((x, after))[0]


def mm(a, b):
    return jnp.dot(a, b, preferred_element_type=F32)


def mm_nt(a, b):
    return lax.dot_general(a, b, (((1,), (1,)), ((), ())), preferred_element_type=F32)


def mm_tn(a, b):
    return lax.dot_general(a, b, (((0,), (0,)), ((), ())), preferred_element_type=F32)


def norm_factor(u):
    return lax.rsqrt(jnp.mean(u * u, axis=0, keepdims=True) + EPSILON)


def rotate_forward(u, gain, cos, sin):
    n = u * norm_factor(u) * gain
    half = n.shape[0] // 2
    a, b = n[:half], n[half:]
    return jnp.concatenate([a * cos - b * sin, b * cos + a * sin], axis=0)


def rotate_backward(grad, u, gain, cos, sin):
    half = u.shape[0] // 2
    a, b = grad[:half], grad[half:]
    inner = jnp.concatenate([a * cos + b * sin, b * cos - a * sin], axis=0) * gain
    factor = norm_factor(u)
    along = jnp.mean(inner * u, axis=0, keepdims=True)
    return factor * (inner - u * (factor * factor * along))


def visible_weights(score, place, first, rows_at, scale):
    rows = first.shape[1]
    keys = score.shape[0]
    key = place + lax.broadcasted_iota(jnp.int32, (keys, rows), 0)
    row = rows_at + lax.broadcasted_iota(jnp.int32, (keys, rows), 1)
    seen = (key >= first) & (key <= row)
    heads = score.shape[1] // rows
    return jnp.concatenate(
        [
            jnp.where(seen, jnp.exp(score[:, h * rows : (h + 1) * rows] * scale), 0.0)
            for h in range(heads)
        ],
        axis=1,
    )


def keys_kernel(me_ref, *refs, count):
    pieces, (gain_ref, cos_ref, sin_ref, proj_ref, kv_ref) = refs[:count], refs[count:]
    rows = pieces[0].shape[0]
    for bits in range(count):
        at = pl.multiple_of((me_ref[0] ^ bits) * rows, 8)
        proj_ref[pl.ds(at, rows), :] = pieces[bits][...]
    hd = gain_ref.shape[0]
    low = proj_ref.shape[0] - 2 * hd
    key = rotate_forward(proj_ref[low : low + hd, :], gain_ref[...], cos_ref[...], sin_ref[...])
    kv_ref[:hd, :] = key.astype(BF)
    kv_ref[hd:, :] = proj_ref[low + hd :, :].astype(BF)


def own_kernel(me_ref, proj_ref, kv_ref, gain_ref, cos_ref, sin_ref, first_ref, up_ref,
               q_ref, weight_ref, prob_ref, sum_ref, den_ref):
    hd = gain_ref.shape[0]
    rows = proj_ref.shape[1]
    heads = proj_ref.shape[0] // hd - 2
    scale = 1.0 / math.sqrt(hd)
    for h in range(heads):
        q_ref[:, h * rows : (h + 1) * rows] = rotate_forward(
            proj_ref[h * hd : (h + 1) * hd, :], gain_ref[...], cos_ref[...], sin_ref[...]
        ).astype(BF)
    score = mm_tn(kv_ref[:hd, :], q_ref[...])
    at = me_ref[0] * rows
    weight = visible_weights(score, at, first_ref[...], at, scale)
    weight_ref[...] = weight
    den_ref[...] = jnp.sum(weight, axis=0, keepdims=True)
    sum_ref[...] = mm(kv_ref[hd:, :], weight.astype(BF))
    prob_ref[...] = mm_tn(kv_ref[hd:, :], up_ref[...])


def block_backward(weight, grad_prob, inverse, delta, scale, q, up):
    prob = weight * inverse
    grad_score = (prob * (grad_prob - delta) * scale).astype(BF)
    grad_key = mm_nt(q, grad_score)
    grad_value = mm_nt(up, prob.astype(BF))
    return grad_score, grad_key, grad_value


def far_kernel(me_ref, *refs, span, hd):
    windows = refs[:span]
    first_ref, up_ref, q_ref, sum_ref, den_ref = refs[span : span + 5]
    att_ref, gq_ref, inv_ref, delta_ref = refs[span + 5 : span + 9]
    slots = refs[span + 9 :]
    rows = first_ref.shape[1]
    heads = q_ref.shape[1] // rows
    scale = 1.0 / math.sqrt(hd)
    total, den = sum_ref[...], den_ref[...]
    weights = []
    for distance in range(1, span + 1):
        kv = windows[distance - 1]
        score = mm_tn(kv[:hd, :], q_ref[...])
        weight = visible_weights(
            score, (me_ref[0] - distance) * rows, first_ref[...], me_ref[0] * rows, scale
        )
        den = den + jnp.sum(weight, axis=0, keepdims=True)
        total = total + mm(kv[hd:, :], weight.astype(BF))
        weights.append(weight)
    inverse = 1.0 / den
    attended = (total * inverse).astype(BF).astype(F32)
    delta = jnp.sum(up_ref[...].astype(F32) * attended, axis=0, keepdims=True)
    for h in range(heads):
        att_ref[:, h * hd : (h + 1) * hd] = attended[:, h * rows : (h + 1) * rows].T.astype(BF)
    grad_query = jnp.zeros(gq_ref.shape, F32)
    for distance in range(1, span + 1):
        kv = windows[distance - 1]
        grad_score, grad_key, grad_value = block_backward(
            weights[distance - 1],
            mm_tn(kv[hd:, :], up_ref[...]),
            inverse,
            delta,
            scale,
            q_ref[...],
            up_ref[...],
        )
        grad_query = grad_query + mm(kv[:hd, :], grad_score)
        slots[distance - 1][:hd, :] = grad_key.astype(BF)
        slots[distance - 1][hd:, :] = grad_value.astype(BF)
    gq_ref[...] = grad_query
    inv_ref[...] = inverse
    delta_ref[...] = delta


def near_kernel(proj_ref, kv_ref, gain_ref, cos_ref, sin_ref, up_ref, q_ref, weight_ref, prob_ref,
                gq_ref, inv_ref, delta_ref, out_ref, slot_ref):
    hd = gain_ref.shape[0]
    rows = proj_ref.shape[1]
    heads = proj_ref.shape[0] // hd - 2
    scale = 1.0 / math.sqrt(hd)
    grad_score, grad_key, grad_value = block_backward(
        weight_ref[...], prob_ref[...], inv_ref[...], delta_ref[...], scale, q_ref[...], up_ref[...]
    )
    slot_ref[:hd, :] = grad_key
    slot_ref[hd:, :] = grad_value
    grad_query = gq_ref[...] + mm(kv_ref[:hd, :], grad_score)
    for h in range(heads):
        out_ref[h * hd : (h + 1) * hd, :] = rotate_backward(
            grad_query[:, h * rows : (h + 1) * rows],
            proj_ref[h * hd : (h + 1) * hd, :],
            gain_ref[...],
            cos_ref[...],
            sin_ref[...],
        ).astype(BF)


def pair_kernel(slot_ref, *refs, count):
    arrived = refs[:count]
    proj_ref, gain_ref, cos_ref, sin_ref, out_ref = refs[count:]
    hd = gain_ref.shape[0]
    total = slot_ref[...]
    for part in arrived:
        total = total + part[...].astype(F32)
    low = proj_ref.shape[0] - 2 * hd
    out_ref[:hd, :] = rotate_backward(
        total[:hd], proj_ref[low : low + hd, :], gain_ref[...], cos_ref[...], sin_ref[...]
    ).astype(BF)
    out_ref[hd:, :] = total[hd:].astype(BF)


def by_bits(n):
    return n >= 2 and n & (n - 1) == 0 and n <= 8


def far_first(n):
    return sorted(range(0, n, 2), key=lambda b: -bin(b).count("1"))


def gather_pieces(shard, n):
    if not by_bits(n):
        return [lax.all_gather(shard, "dp", axis=0, tiled=True)]
    pieces = {0: shard}
    for bits in far_first(n)[:-1]:
        pieces[bits] = swap(shard, "dp", bits)
    for bits in range(0, n, 2):
        pieces[bits | 1] = swap(pieces[bits], "dp", 1)
    return [pieces[bits] for bits in range(n)]


def weights_kernel(me_ref, side_ref, *refs, count, heads_rows, groups):
    pieces, (mine_ref, give_ref, whole_ref) = refs[:count], refs[count:]
    rows = pieces[0].shape[0]
    for bits in range(count):
        at = pl.multiple_of((me_ref[0] ^ bits) * rows, rows)
        whole_ref[pl.ds(at, rows), :] = pieces[bits][...]
    width = whole_ref.shape[1] // groups
    half = give_ref.shape[0]
    low = pl.multiple_of(lax.rem(me_ref[1], heads_rows // half) * half, half)
    for k in range(groups // 2):
        mine = pl.multiple_of((2 * k + side_ref[0]) * width, 128)
        give = pl.multiple_of((2 * k + 1 - side_ref[0]) * width, 128)
        to = slice(k * width, (k + 1) * width)
        mine_ref[:, to] = whole_ref[:, pl.ds(mine, width)]
        give_ref[:, to] = whole_ref[pl.ds(low, half), pl.ds(give, width)]


def token_q_kernel(me_ref, own_ref, their_ref, mine_ref, *refs):
    given, out_ref = refs[:-1], refs[-1]
    rows = own_ref.shape[0]
    total = mm_tn(own_ref[...], mine_ref[:rows, :])
    half = given[0].shape[0]
    for at, part in enumerate(given):
        low = pl.multiple_of(lax.rem(me_ref[0] + at, len(given)) * half, half)
        total = total + mm_tn(their_ref[pl.ds(low, half), :], part[...])
    out_ref[...] = total


def token_kv_kernel(pair_ref, so_far_ref, own_ref, their_ref, mine_ref, both_ref, keep_ref, *refs):
    sends, total_ref = refs[:-1], refs[-1]
    both = (own_ref[...].astype(F32) + their_ref[...].astype(F32)).astype(BF)
    both_ref[...] = both
    low = mine_ref.shape[0] - both.shape[0]
    total_ref[...] = so_far_ref[...] + mm_tn(both, mine_ref[low:, :])
    width = keep_ref.shape[1]
    pairs = len(sends) + 1
    chunk = lambda by: total_ref[
        :, pl.ds(pl.multiple_of(lax.rem(pair_ref[0] + by, pairs) * width, 128), width)
    ]
    keep_ref[...] = chunk(0)
    for by in range(1, pairs):
        sends[by - 1][...] = chunk(by).astype(BF)


def parts_kernel(me_ref, own_q, own_kv, other_q, other_kv, tokens_ref, other_ref, *refs, order):
    outs, (rows_ref, all_ref) = refs[:-2], refs[-2:]
    low, width = own_q.shape
    all_ref[:low, :width] = own_q[...]
    all_ref[low:, :width] = own_kv[...]
    all_ref[:low, width:] = other_q[...]
    all_ref[low:, width:] = other_kv[...]
    rows = outs[0].shape[0]
    for at, bits in enumerate(order):
        start = pl.multiple_of((me_ref[0] ^ bits) * rows, 16)
        rows_ref[at * rows : (at + 1) * rows, :] = all_ref[pl.ds(start, rows), :]
    product = mm(rows_ref[:, :width], tokens_ref[...]) + mm(rows_ref[:, width:], other_ref[...])
    for at, out in enumerate(outs):
        out[...] = product[at * rows : (at + 1) * rows].astype(out.dtype)


def step(tokens, weights, query_gain, key_gain, first_row, cotangent):
    hd = query_gain.shape[0]
    rows = tokens.shape[0]
    n = lax.axis_size("dp")
    cols = weights.shape[1] * n
    heads = cols // hd - 2
    span = -(-MOST // rows)
    me = lax.axis_index("dp")
    where = me.astype(jnp.int32).reshape(1)
    lanes = heads * rows
    position = (me * rows + jnp.arange(rows, dtype=jnp.int32)).astype(F32) * STRETCH
    channel = jnp.arange(hd // 2, dtype=F32)
    angles = (THETA ** (-2.0 * channel / hd))[:, None] * position[None, :]
    cos, sin = jnp.cos(angles), jnp.sin(angles)
    q_gain, k_gain = query_gain.reshape(hd, 1), key_gain.reshape(hd, 1)
    first = first_row.reshape(1, rows)
    up = cotangent.reshape(rows, heads, hd).transpose(2, 1, 0).reshape(hd, lanes)

    pieces = gather_pieces(weights[0], n)
    other_tokens = swap(tokens, "dp", 1) if by_bits(n) else None
    parts = [mm_nt(piece, tokens) for piece in pieces]
    if len(parts) == 1:
        where_keys = jnp.zeros((1,), jnp.int32)
    else:
        where_keys = where
    unit = 2 * rows * lanes * hd
    proj, kv = on_core(
        lambda *r: keys_kernel(*r, count=len(parts)),
        [((cols, rows), F32), ((2 * hd, rows), BF)],
        [where_keys, *parts, k_gain, cos, sin],
        unit,
        after=[up, q_gain, first],
    )
    windows = [from_behind(kv, "dp", distance) for distance in range(1, span + 1)]
    q, weight_own, prob_own, sum_own, den_own = on_core(
        own_kernel,
        [((hd, lanes), BF), ((rows, lanes), F32), ((rows, lanes), F32), ((hd, lanes), F32),
         ((1, lanes), F32)],
        [where, proj, kv, q_gain, cos, sin, first, up],
        4 * unit,
    )
    n_head = lax.axis_size("head")
    g = lax.axis_index("head").astype(jnp.int32)
    pairs = n_head // 2
    split = 2 if by_bits(n) else 1
    q_rows = heads * hd
    width = tokens.shape[1] // n_head
    mine, give = on_core(
        lambda *r: weights_kernel(*r, count=len(pieces), heads_rows=q_rows, groups=n_head),
        [((cols, pairs * width), BF), ((q_rows // split, pairs * width), BF)],
        [jnp.concatenate([where_keys, where]), lax.rem(g, 2).reshape(1), *pieces],
        unit,
        [pltpu.VMEM((cols, tokens.shape[1]), BF)],
        after=[kv],
    )
    given = [swap(give, "head", 1)]
    attended, grad_query, inverse, delta, *slots = on_core(
        lambda *r: far_kernel(*r, span=span, hd=hd),
        [((rows, heads * hd), BF), ((hd, lanes), F32), ((1, lanes), F32), ((1, lanes), F32)]
        + [((2 * hd, rows), BF)] * span,
        [where, *windows, first, up, q, sum_own, den_own],
        12 * unit,
        mib=28,
    )
    arrived = [
        from_behind(slot, "dp", -distance) for distance, slot in zip(range(1, span + 1), slots)
    ]
    grad_q, slot_own = on_core(
        near_kernel,
        [((heads * hd, rows), BF), ((2 * hd, rows), F32)],
        [proj, kv, q_gain, cos, sin, up, q, weight_own, prob_own, grad_query, inverse, delta],
        4 * unit,
    )
    (grad_kv,) = on_core(
        lambda *r: pair_kernel(*r, count=span),
        [((2 * hd, rows), BF)],
        [slot_own, *arrived, proj, k_gain, cos, sin],
        unit,
    )
    if split == 2:
        given.append(swap(later(given[0], grad_q), "dp", 1))
    their_q = swap(grad_q, "head", 1)
    their_kv = swap(grad_kv, "head", 1)
    (so_far,) = on_core(
        token_q_kernel,
        [((rows, pairs * width), F32)],
        [where, grad_q, their_q, mine, *given],
        4 * unit,
    )
    both, token_grad, *sends = on_core(
        token_kv_kernel,
        [((2 * hd, rows), BF), ((rows, width), F32)] + [((rows, width), BF)] * (pairs - 1),
        [lax.div(g, 2).reshape(1), so_far, grad_kv, their_kv, mine],
        unit,
        [pltpu.VMEM((rows, pairs * width), F32)],
    )
    summed = [rotate(part, "head", 2 * by) for by, part in enumerate(sends, 1)]
    if by_bits(n):
        other_q = swap(grad_q, "dp", 1)
        other_kv = swap(both, "dp", 1)
        order = far_first(n)
        shard = cols // n
        *going, weight_grad = on_core(
            lambda *r: parts_kernel(*r, order=order),
            [((shard, tokens.shape[1]), F32 if bits == 0 else BF) for bits in order],
            [where, grad_q, both, other_q, other_kv, tokens, other_tokens],
            4 * unit,
            [pltpu.VMEM((len(order) * shard, 2 * rows), BF), pltpu.VMEM((cols, 2 * rows), BF)],
        )
        for bits, part in zip(order, going):
            weight_grad = weight_grad + swap(part, "dp", bits).astype(F32)
    else:
        weight_grad = lax.psum_scatter(
            mm(jnp.concatenate([grad_q, both], axis=0), tokens),
            "dp",
            scatter_dimension=0,
            tiled=True,
        )
    for part in summed:
        token_grad = token_grad + part.astype(F32)
    return (attended, token_grad.astype(BF), weight_grad[None])


def solution(mesh):
    in_specs = (P("dp", None), P("head", "dp", None), P(), P(), P("dp"), P("dp", "head"))
    out_specs = (P("dp", "head"), P("dp", "head"), P("head", "dp", None))
    return jax.shard_map(step, mesh=mesh, in_specs=in_specs, out_specs=out_specs, check_vma=False)
```

time: 186 us -> 87.3 us (0.47)
  waiting for transfers between devices: 127 us -> 43.6 us
  between operations: 14.1 us -> 1.02 us
  starting transfers between devices: 10.4 us -> 23.3 us
  matrix products: 16.7 us -> 5.1 us
  Pallas kernels: 0 us -> 10.3 us
  other arithmetic: 11.9 us -> 2.25 us
  local copies, waits for them, and re-layouts: 5.22 us -> 1.31 us
    reduce_scatter x2 -> x0, waiting for transfers between devices: 73.4 us -> none  [the longest x1 59.1 us: body(): lax.psum_scatter(jnp.einsum('rc,rd->cd', grad_projected, tokens, preferre...]
    all_gather x1 -> x0, waiting for transfers between devices: 33.3 us -> none  [body(): weight_piece = lax.all_gather(weights, 'dp', axis=1, tiled=True)]
    ppermute x5 -> x22, waiting for transfers between devices: 19.8 us -> 43.6 us  [the longest x17 28.5 us: swap(): lax.ppermute(x, axis, [(i, i ^ bits) for i in range(lax.axis_size(axis))])]
    ppermute x5 -> x22, starting transfers between devices: 10.3 us -> 23.3 us  [the longest x17 13.6 us: swap(): lax.ppermute(x, axis, [(i, i ^ bits) for i in range(lax.axis_size(axis))])]
    dot_general x9 -> x8, matrix products: 16.7 us -> 5.1 us  [mm_nt(): lax.dot_general(a, b, (((1,), (1,)), ((), ())), preferred_element_type=F32)]
    pallas_call x0 -> x9, Pallas kernels: none -> 10.3 us  [on_core(): pl.pallas_call(run, out_shape=[jax.ShapeDtypeStruct(s, d) for s, d in out...]
    unnamed x16 -> x25, local copies, waits for them, and re-layouts: 2.68 us -> 0.79 us
  transfers between devices with their start and end apart: 8 -> 22, of which waited for: 7 -> 10; matrix products, arithmetic and copies ran while one was open for 8% -> 7% of each run, Pallas kernels for 0% -> 11%
where the time goes in v1:
time: 87.3 us; the launch traced here: 87 us
  waiting for transfers between devices  43.6 us (50%)
  starting transfers between devices  23.3 us (27%)
  Pallas kernels  10.3 us (12%)
  matrix products  5.1 us (6%)
  other arithmetic  2.25 us (3%)
  local copies, waits for them, and re-layouts  1.31 us (2%)
  between operations  1.02 us (1%)
    ppermute x17, waiting for transfers between devices, swap(): lax.ppermute(x, axis, [(i, i ^ bits) for i in range(lax.axis_size(axis))])  28.5 us
    ppermute x17, starting transfers between devices, swap(): lax.ppermute(x, axis, [(i, i ^ bits) for i in range(lax.axis_size(axis))])  13.6 us
    pallas_call x9, Pallas kernels, on_core(): pl.pallas_call(run, out_shape=[jax.ShapeDtypeStruct(s, d) for s, d in out...  10.3 us
    ppermute x4, waiting for transfers between devices, from_behind(): lax.ppermute(x, axis, [(i, i + by) for i in range(n) if 0 <= i + by < n])  8.76 us
    ppermute x4, starting transfers between devices, from_behind(): lax.ppermute(x, axis, [(i, i + by) for i in range(n) if 0 <= i + by < n])  7.06 us
    ppermute x1, waiting for transfers between devices, rotate(): return lax.ppermute(x, axis, [(i, (i + by) % n) for i in range(n)])  6.4 us
    dot_general x8, matrix products, mm_nt(): lax.dot_general(a, b, (((1,), (1,)), ((), ())), preferred_element_type=F32)  5.1 us
    ppermute x1, starting transfers between devices, rotate(): return lax.ppermute(x, axis, [(i, (i + by) % n) for i in range(n)])  2.66 us
  transfers between devices with their start and end apart: 22, of which 10 were waited for; matrix products, arithmetic and copies ran while one was open for 7% of the time, Pallas kernels for 11%

profile of v1, /device:TPU:0, one launch (start us, length us, event | category | flops | bytes accessed | tf_op | source)
XLA Modules:
  0.0 87.0 jit_solution(18289082478964970380)
XLA Ops:
  0.6 3.0 %collective-permute-start.1 = (bf16[96,2048]{1,0:T(8,128)(2,1)}, bf16[96,2048]{1,0:T(8,128)(2,1)S(1)}, u32[]{:S(2)}, u32[]{:S(2)}) collective-permute-start(bf16[96,2048]{1,0:T(8,128)(2,1)} %bitcast.33), channel_id=1, source_target_pairs={{0,8},{4,12},{8,0},{12,4},{16,24},{20,28},{24,16},{28,20},{1,9},{5... | collective-permute-start | bytes 1179656 | tf_op jit(solution)/shard_map/ppermute | solution.py:20
  3.7 1.5 %collective-permute-start.3 = (bf16[96,2048]{1,0:T(8,128)(2,1)}, bf16[96,2048]{1,0:T(8,128)(2,1)S(1)}, u32[]{:S(2)}, u32[]{:S(2)}) collective-permute-start(bf16[96,2048]{1,0:T(8,128)(2,1)} %bitcast.34), channel_id=1, source_target_pairs={{0,16},{4,20},{8,24},{12,28},{16,0},{20,4},{24,8},{28,12},{1,17},{... | collective-permute-start | bytes 1179656 | tf_op jit(solution)/shard_map/ppermute | solution.py:20
  5.3 1.9 %fusion.refs_1_ = f32[96,256]{1,0:T(8,128)S(1)} fusion(bf16[256,2048]{1,0:T(8,128)(2,1)} %refs_5_.1, bf16[1,96,2048]{2,1,0:T(8,128)(2,1)} %param.7), kind=kOutput, calls=%fused_computation.7 | convolution fusion | flops 100663296 | bytes 1540096 | tf_op jit(solution)/shard_map/dot_general | solution.py:63
  8.1 5.7 %collective-permute-done.1.refs_4_ = bf16[96,2048]{1,0:T(8,128)(2,1)S(1)} collective-permute-done((bf16[96,2048]{1,0:T(8,128)(2,1)}, bf16[96,2048]{1,0:T(8,128)(2,1)S(1)}, u32[]{:S(2)}, u32[]{:S(2)}) %collective-permute-start.1) | collective-permute-done | bytes 393248 | tf_op jit(solution)/shard_map/ppermute | solution.py:20
  14.3 8.6 %collective-permute-done.3.refs_6_ = bf16[96,2048]{1,0:T(8,128)(2,1)S(1)} collective-permute-done((bf16[96,2048]{1,0:T(8,128)(2,1)}, bf16[96,2048]{1,0:T(8,128)(2,1)S(1)}, u32[]{:S(2)}, u32[]{:S(2)}) %collective-permute-start.3) | collective-permute-done | bytes 393248 | tf_op jit(solution)/shard_map/ppermute | solution.py:20
  23.4 0.6 collective-permute-start.6
  27.3 0.9 %shard_map.89 = (bf16[768,1024]{1,0:T(8,128)(2,1)S(1)}, bf16[256,1024]{1,0:T(8,128)(2,1)S(1)}) custom-call(s32[2]{0:T(128)S(1)} %pad_add_fusion.refs_0_, s32[1]{0:T(128)} %bitcast.7.refs_1_, bf16[96,2048]{1,0:T(8,128)(2,1)S(1)} %bitcast.37, bf16[96,2048]{1,0:T(8,128)(2,1)S(1)} %copy-done.7, bf16[96,2048]{1,0:T(8,128)(2,1)S(1)} %collective-permute-done.1.refs_4_, ...), custom_call_target="tpu_custom_call" | custom-call | flops 67108864 | bytes 1048576 | tf_op jit(solution)/shard_map/pallas_call | solution.py:43
  28.2 1.6 %collective-permute-start.10 = (bf16[256,1024]{1,0:T(8,128)(2,1)S(1)}, bf16[256,1024]{1,0:T(8,128)(2,1)}, u32[]{:S(2)}, u32[]{:S(2)}) collective-permute-start(bf16[256,1024]{1,0:T(8,128)(2,1)S(1)} %get-tuple-element.41), channel_id=1, source_target_pairs={{0,1},{1,0},{2,3},{3,2},{4,5},{5,4},{6,7},{7,6},{8,9},{9,8},{10,11... | collective-permute-start | bytes 1572872 | tf_op jit(solution)/shard_map/ppermute | solution.py:20
  29.8 2.4 %collective-permute-start.7 = (bf16[256,256]{1,0:T(8,128)(2,1)S(1)}, bf16[256,256]{1,0:T(8,128)(2,1)S(1)}, u32[]{:S(2)}, u32[]{:S(2)}) collective-permute-start(bf16[256,256]{1,0:T(8,128)(2,1)S(1)} %get-tuple-element.28.refs_2_.refs_1_.refs_10_), channel_id=1, source_target_pairs={{0,4},{4,8},{8,12},{12,16},{16,20},{20,24},{24,28},{1,5},{5,9},{9,... | collective-permute-start | bytes 393224 | tf_op jit(solution)/shard_map/ppermute | solution.py:30
  32.2 2.1 %collective-permute-start.8 = (bf16[256,256]{1,0:T(8,128)(2,1)S(1)}, bf16[256,256]{1,0:T(8,128)(2,1)S(1)}, u32[]{:S(2)}, u32[]{:S(2)}) collective-permute-start(bf16[256,256]{1,0:T(8,128)(2,1)S(1)} %get-tuple-element.28.refs_2_.refs_1_.refs_10_), channel_id=1, source_target_pairs={{0,8},{4,12},{8,16},{12,20},{16,24},{20,28},{1,9},{5,13},{9,17},{1... | collective-permute-start | bytes 393224 | tf_op jit(solution)/shard_map/ppermute | solution.py:30
  34.3 0.8 shard_map.86
  35.2 1.6 %collective-permute-done.8.refs_2_ = bf16[256,256]{1,0:T(8,128)(2,1)S(1)} collective-permute-done((bf16[256,256]{1,0:T(8,128)(2,1)S(1)}, bf16[256,256]{1,0:T(8,128)(2,1)S(1)}, u32[]{:S(2)}, u32[]{:S(2)}) %collective-permute-start.8) | collective-permute-done | bytes 131104 | tf_op jit(solution)/shard_map/ppermute | solution.py:30
  36.8 2.8 %shard_map.87 = (bf16[256,512]{1,0:T(8,128)(2,1)}, f32[128,1024]{1,0:T(8,128)S(1)}, f32[1,1024]{1,0:T(1,128)S(1)}, f32[1,1024]{1,0:T(1,128)S(1)}, bf16[256,256]{...) custom-call(s32[1]{0:T(128)} %bitcast.refs_0_, bf16[256,256]{1,0:T(8,128)(2,1)S(1)} %collective-permute-done.7.refs_1_, ...), custom_call_target="tpu_custom_call" | custom-call | flops 805306368 | bytes 1048576 | tf_op jit(solution)/shard_map/pallas_call | solution.py:43
  39.6 0.8 shard_map.88
  40.5 1.7 %collective-permute-done.10.refs_4_ = bf16[256,1024]{1,0:T(8,128)(2,1)} collective-permute-done((bf16[256,1024]{1,0:T(8,128)(2,1)S(1)}, bf16[256,1024]{1,0:T(8,128)(2,1)}, u32[]{:S(2)}, u32[]{:S(2)}) %collective-permute-start.10) | collective-permute-done | bytes 524320 | tf_op jit(solution)/shard_map/ppermute | solution.py:20
  42.2 1.6 %collective-permute-start.9 = (bf16[512,256]{1,0:T(8,128)(2,1)S(1)}, bf16[512,256]{1,0:T(8,128)(2,1)}, u32[]{:S(2)}, u32[]{:S(2)}) collective-permute-start(bf16[512,256]{1,0:T(8,128)(2,1)S(1)} %get-tuple-element.39.refs_1_), channel_id=1, source_target_pairs={{0,1},{1,0},{2,3},{3,2},{4,5},{5,4},{6,7},{7,6},{8,9},{9,8},{10,11... | collective-permute-start | bytes 786440 | tf_op jit(solution)/shard_map/ppermute | solution.py:20
  43.8 1.3 %collective-permute-start.12 = (bf16[256,256]{1,0:T(8,128)(2,1)S(1)}, bf16[256,256]{1,0:T(8,128)(2,1)S(1)}, u32[]{:S(2)}, u32[]{:S(2)}) collective-permute-start(bf16[256,256]{1,0:T(8,128)(2,1)S(1)} %get-tuple-element.44), channel_id=1, source_target_pairs={{4,0},{8,4},{12,8},{16,12},{20,16},{24,20},{28,24},{5,1},{9,5},{13... | collective-permute-start | bytes 393224 | tf_op jit(solution)/shard_map/ppermute | solution.py:30
  45.1 1.3 %collective-permute-start.13 = (bf16[256,256]{1,0:T(8,128)(2,1)S(1)}, bf16[256,256]{1,0:T(8,128)(2,1)S(1)}, u32[]{:S(2)}, u32[]{:S(2)}) collective-permute-start(bf16[256,256]{1,0:T(8,128)(2,1)S(1)} %get-tuple-element.45), channel_id=1, source_target_pairs={{8,0},{12,4},{16,8},{20,12},{24,16},{28,20},{9,1},{13,5},{17,9},{2... | collective-permute-start | bytes 393224 | tf_op jit(solution)/shard_map/ppermute | solution.py:30
  46.4 0.6 collective-permute-done.12.refs_1_
  47.0 6.5 %collective-permute-done.13.refs_2_ = bf16[256,256]{1,0:T(8,128)(2,1)S(1)} collective-permute-done((bf16[256,256]{1,0:T(8,128)(2,1)S(1)}, bf16[256,256]{1,0:T(8,128)(2,1)S(1)}, u32[]{:S(2)}, u32[]{:S(2)}) %collective-permute-start.13) | collective-permute-done | bytes 131104 | tf_op jit(solution)/shard_map/ppermute | solution.py:30
  53.6 1.2 %collective-permute-start.14 = (bf16[256,256]{1,0:T(8,128)(2,1)S(1)}, bf16[256,256]{1,0:T(8,128)(2,1)S(1)}, u32[]{:S(2)}, u32[]{:S(2)}) collective-permute-start(bf16[256,256]{1,0:T(8,128)(2,1)S(1)} %shard_map.91.refs_2_), channel_id=1, source_target_pairs={{0,1},{1,0},{2,3},{3,2},{4,5},{5,4},{6,7},{7,6},{8,9},{9,8},{10,11... | collective-permute-start | bytes 393224 | tf_op jit(solution)/shard_map/ppermute | solution.py:20
  54.9 2.0 %shard_map.90.refs_1_ = f32[256,1024]{1,0:T(8,128)S(1)} custom-call(s32[1]{0:T(128)} %bitcast.refs_0_, bf16[512,256]{1,0:T(8,128)(2,1)S(1)} %get-tuple-element.39.refs_1_, bf16[512,256]{1,0:T(8,128)(2,1)} %collective-permute-done.9.refs_2_, bf16[768,1024]{1,0:T(8,128)(2,1)S(1)} %get-tuple-element.40.refs_3_.refs_4_, ...), custom_call_target="tpu_custom_call" | custom-call | flops 268435456 | bytes 1048576 | tf_op jit(solution)/shard_map/pallas_call | solution.py:43
  56.9 2.0 %collective-permute-done.14.refs_3_ = bf16[256,256]{1,0:T(8,128)(2,1)S(1)} collective-permute-done((bf16[256,256]{1,0:T(8,128)(2,1)S(1)}, bf16[256,256]{1,0:T(8,128)(2,1)S(1)}, u32[]{:S(2)}, u32[]{:S(2)}) %collective-permute-start.14) | collective-permute-done | bytes 131104 | tf_op jit(solution)/shard_map/ppermute | solution.py:20
  59.5 2.7 %collective-permute-start.15 = (bf16[256,512]{1,0:T(8,128)(2,1)S(1)}, bf16[256,512]{1,0:T(8,128)(2,1)S(1)}, u32[]{:S(2)}, u32[]{:S(2)}) collective-permute-start(bf16[256,512]{1,0:T(8,128)(2,1)S(1)} %get-tuple-element.47), channel_id=1, source_target_pairs={{0,2},{1,3},{2,0},{3,1},{4,6},{5,7},{6,4},{7,5},{8,10},{9,11},{10,... | collective-permute-start | bytes 786440 | tf_op jit(solution)/shard_map/ppermute | solution.py:25
  62.1 2.2 %shard_map.93 = (bf16[96,2048]{1,0:T(8,128)(2,1)S(1)}, bf16[96,2048]{1,0:T(8,128)(2,1)S(1)}, bf16[96,2048]{1,0:T(8,128)(2,1)S(1)}, f32[96,2048]{1,0:T(8,128)S(1)}) custom-call(s32[1]{0:T(128)} %bitcast.refs_0_, bf16[512,256]{1,0:T(8,128)(2,1)S(1)} %get-tuple-element.39.refs_1_, bf16[256,256]{1,0:T(8,128)(2,1)S(1)} %get-tuple-element.48.refs_2_, ...), custom_call_target="tpu_custom_call" | custom-call | flops 268435456 | bytes 1048576 | tf_op jit(solution)/shard_map/pallas_call | solution.py:43
  64.4 1.4 %collective-permute-start.19 = (bf16[96,2048]{1,0:T(8,128)(2,1)S(1)}, bf16[96,2048]{1,0:T(8,128)(2,1)S(1)}, u32[]{:S(2)}, u32[]{:S(2)}) collective-permute-start(bf16[96,2048]{1,0:T(8,128)(2,1)S(1)} %get-tuple-element.50), channel_id=1, source_target_pairs={{0,24},{4,28},{8,16},{12,20},{16,8},{20,12},{24,0},{28,4},{1,25},{... | collective-permute-start | bytes 1179656 | tf_op jit(solution)/shard_map/ppermute | solution.py:20
  65.8 2.5 %collective-permute-start.20 = (bf16[96,2048]{1,0:T(8,128)(2,1)S(1)}, bf16[96,2048]{1,0:T(8,128)(2,1)S(1)}, u32[]{:S(2)}, u32[]{:S(2)}) collective-permute-start(bf16[96,2048]{1,0:T(8,128)(2,1)S(1)} %get-tuple-element.51), channel_id=1, source_target_pairs={{0,8},{4,12},{8,0},{12,4},{16,24},{20,28},{24,16},{28,20},{1,9},{5... | collective-permute-start | bytes 1179656 | tf_op jit(solution)/shard_map/ppermute | solution.py:20
  68.3 6.4 %collective-permute-done.15 = bf16[256,512]{1,0:T(8,128)(2,1)S(1)} collective-permute-done((bf16[256,512]{1,0:T(8,128)(2,1)S(1)}, bf16[256,512]{1,0:T(8,128)(2,1)S(1)}, u32[]{:S(2)}, u32[]{:S(2)}) %collective-permute-start.15) | collective-permute-done | bytes 262176 | tf_op jit(solution)/shard_map/ppermute | solution.py:25
  74.7 0.8 add_convert_fusion
  75.5 1.9 %collective-permute-done.19 = bf16[96,2048]{1,0:T(8,128)(2,1)S(1)} collective-permute-done((bf16[96,2048]{1,0:T(8,128)(2,1)S(1)}, bf16[96,2048]{1,0:T(8,128)(2,1)S(1)}, u32[]{:S(2)}, u32[]{:S(2)}) %collective-permute-start.19) | collective-permute-done | bytes 393248 | tf_op jit(solution)/shard_map/ppermute | solution.py:20
  77.4 8.5 %collective-permute-done.20 = bf16[96,2048]{1,0:T(8,128)(2,1)S(1)} collective-permute-done((bf16[96,2048]{1,0:T(8,128)(2,1)S(1)}, bf16[96,2048]{1,0:T(8,128)(2,1)S(1)}, u32[]{:S(2)}, u32[]{:S(2)}) %collective-permute-start.20) | collective-permute-done | bytes 393248 | tf_op jit(solution)/shard_map/ppermute | solution.py:20
  85.9 1.1 %add_bitcast_fusion = f32[1,96,2048]{2,1,0:T(8,128)} fusion(bf16[96,2048]{1,0:T(8,128)(2,1)S(1)} %collective-permute-done.21, bf16[96,2048]{1,0:T(8,128)(2,1)S(1)} %collective-permute-done.20, f32[96,2048]{1,0:T(8,128)S(1)} %get-tuple-element.49, bf16[96,2048]{1,0:T(8,128)(2,1)S(1)} %collective-permute-done.19), kind=kLoop, calls=%fused_computation | loop fusion | flops 1179648 | bytes 2752512 | tf_op jit(solution)/shard_map/broadcast_in_dim | solution.py:425
  (64 shorter events, 5.8 us)
Async XLA Ops:
  0.6 6.9 %copy-start.9 = (bf16[256,512]{1,0:T(8,128)(2,1)S(1)}, bf16[256,512]{1,0:T(8,128)(2,1)}, u32[]{:S(2)}) copy-start(bf16[256,512]{1,0:T(8,128)(2,1)} %param.11) | copy-start | bytes 786436
  0.6 13.2 %collective-permute-start.1 = (bf16[96,2048]{1,0:T(8,128)(2,1)}, bf16[96,2048]{1,0:T(8,128)(2,1)S(1)}, u32[]{:S(2)}, u32[]{:S(2)}) collective-permute-start(bf16[96,2048]{1,0:T(8,128)(2,1)} %bitcast.33), channel_id=1, source_target_pairs={{0,8},{4,12},{8,0},{12,4},{16,24},{20,28},{24,16},{28,20},{1,9},{5... | collective-permute-start | bytes 1179656 | tf_op jit(solution)/shard_map/ppermute | solution.py:20
  3.7 19.2 %collective-permute-start.3 = (bf16[96,2048]{1,0:T(8,128)(2,1)}, bf16[96,2048]{1,0:T(8,128)(2,1)S(1)}, u32[]{:S(2)}, u32[]{:S(2)}) collective-permute-start(bf16[96,2048]{1,0:T(8,128)(2,1)} %bitcast.34), channel_id=1, source_target_pairs={{0,16},{4,20},{8,24},{12,28},{16,0},{20,4},{24,8},{28,12},{1,17},{... | collective-permute-start | bytes 1179656 | tf_op jit(solution)/shard_map/ppermute | solution.py:20
  5.2 18.2 %collective-permute-start.5 = (bf16[96,2048]{1,0:T(8,128)(2,1)}, bf16[96,2048]{1,0:T(8,128)(2,1)S(1)}, u32[]{:S(2)}, u32[]{:S(2)}) collective-permute-start(bf16[96,2048]{1,0:T(8,128)(2,1)} %bitcast.35), channel_id=1, source_target_pairs={{0,24},{4,28},{8,16},{12,20},{16,8},{20,12},{24,0},{28,4},{1,25},{... | collective-permute-start | bytes 1179656 | tf_op jit(solution)/shard_map/ppermute | solution.py:20
  5.2 19.2 %collective-permute-start = (bf16[96,2048]{1,0:T(8,128)(2,1)}, bf16[96,2048]{1,0:T(8,128)(2,1)S(1)}, u32[]{:S(2)}, u32[]{:S(2)}) collective-permute-start(bf16[96,2048]{1,0:T(8,128)(2,1)} %bitcast.36), channel_id=1, source_target_pairs={{0,4},{4,0},{8,12},{12,8},{16,20},{20,16},{24,28},{28,24},{1,5},{5... | collective-permute-start | bytes 1179656 | tf_op jit(solution)/shard_map/ppermute | solution.py:20
  5.2 2.6 %copy-start.10 = (f32[128]{0:T(128)S(1)}, f32[128]{0:T(128)}, u32[]{:S(2)}) copy-start(f32[128]{0:T(128)} %param.8) | copy-start | bytes 1540
  5.2 2.7 %copy-start.11 = (f32[128]{0:T(128)S(1)}, f32[128]{0:T(128)}, u32[]{:S(2)}) copy-start(f32[128]{0:T(128)} %param.9) | copy-start | bytes 1540
  5.2 8.6 %copy-start = (bf16[256,2048]{1,0:T(8,128)(2,1)S(1)}, bf16[256,2048]{1,0:T(8,128)(2,1)}, u32[]{:S(2)}) copy-start(bf16[256,2048]{1,0:T(8,128)(2,1)} %refs_5_.1) | copy-start | bytes 3145732
  13.8 11.1 %collective-permute-start.2 = (bf16[96,2048]{1,0:T(8,128)(2,1)S(1)}, bf16[96,2048]{1,0:T(8,128)(2,1)S(1)}, u32[]{:S(2)}, u32[]{:S(2)}) collective-permute-start(bf16[96,2048]{1,0:T(8,128)(2,1)S(1)} %collective-permute-done.1.refs_4_), channel_id=1, source_target_pairs={{0,4},{4,0},{8,12},{12,8},{16,20},{20,16},{24,28},{28,24},{1,5},{5... | collective-permute-start | bytes 1179656 | tf_op jit(solution)/shard_map/ppermute | solution.py:20
  22.9 2.0 %copy-start.2 = (bf16[96,2048]{1,0:T(8,128)(2,1)}, bf16[96,2048]{1,0:T(8,128)(2,1)S(1)}, u32[]{:S(2)}) copy-start(bf16[96,2048]{1,0:T(8,128)(2,1)S(1)} %collective-permute-done.3.refs_6_) | copy-start | bytes 1179652
  22.9 2.5 %collective-permute-start.4 = (bf16[96,2048]{1,0:T(8,128)(2,1)S(1)}, bf16[96,2048]{1,0:T(8,128)(2,1)S(1)}, u32[]{:S(2)}, u32[]{:S(2)}) collective-permute-start(bf16[96,2048]{1,0:T(8,128)(2,1)S(1)} %collective-permute-done.3.refs_6_), channel_id=1, source_target_pairs={{0,4},{4,0},{8,12},{12,8},{16,20},{20,16},{24,28},{28,24},{1,5},{5... | collective-permute-start | bytes 1179656 | tf_op jit(solution)/shard_map/ppermute | solution.py:20
  23.4 2.0 %copy-start.4 = (bf16[96,2048]{1,0:T(8,128)(2,1)}, bf16[96,2048]{1,0:T(8,128)(2,1)S(1)}, u32[]{:S(2)}) copy-start(bf16[96,2048]{1,0:T(8,128)(2,1)S(1)} %collective-permute-done.5.refs_8_) | copy-start | bytes 1179652
  23.4 2.6 %collective-permute-start.6 = (bf16[96,2048]{1,0:T(8,128)(2,1)S(1)}, bf16[96,2048]{1,0:T(8,128)(2,1)S(1)}, u32[]{:S(2)}, u32[]{:S(2)}) collective-permute-start(bf16[96,2048]{1,0:T(8,128)(2,1)S(1)} %collective-permute-done.5.refs_8_), channel_id=1, source_target_pairs={{0,4},{4,0},{8,12},{12,8},{16,20},{20,16},{24,28},{28,24},{1,5},{5... | collective-permute-start | bytes 1179656 | tf_op jit(solution)/shard_map/ppermute | solution.py:20
  24.4 1.5 %copy-start.6 = (bf16[96,2048]{1,0:T(8,128)(2,1)}, bf16[96,2048]{1,0:T(8,128)(2,1)S(1)}, u32[]{:S(2)}) copy-start(bf16[96,2048]{1,0:T(8,128)(2,1)S(1)} %collective-permute-done.refs_3_) | copy-start | bytes 1179652
  25.9 1.1 %copy-start.3 = (bf16[96,2048]{1,0:T(8,128)(2,1)S(1)}, bf16[96,2048]{1,0:T(8,128)(2,1)}, u32[]{:S(2)}) copy-start(bf16[96,2048]{1,0:T(8,128)(2,1)} %copy-done.2) | copy-start | bytes 1179652
  25.9 1.2 %copy-start.5 = (bf16[96,2048]{1,0:T(8,128)(2,1)S(1)}, bf16[96,2048]{1,0:T(8,128)(2,1)}, u32[]{:S(2)}) copy-start(bf16[96,2048]{1,0:T(8,128)(2,1)} %copy-done.4) | copy-start | bytes 1179652
  25.9 1.3 %copy-start.7 = (bf16[96,2048]{1,0:T(8,128)(2,1)S(1)}, bf16[96,2048]{1,0:T(8,128)(2,1)}, u32[]{:S(2)}) copy-start(bf16[96,2048]{1,0:T(8,128)(2,1)} %copy-done.6) | copy-start | bytes 1179652
  28.2 14.0 %collective-permute-start.10 = (bf16[256,1024]{1,0:T(8,128)(2,1)S(1)}, bf16[256,1024]{1,0:T(8,128)(2,1)}, u32[]{:S(2)}, u32[]{:S(2)}) collective-permute-start(bf16[256,1024]{1,0:T(8,128)(2,1)S(1)} %get-tuple-element.41), channel_id=1, source_target_pairs={{0,1},{1,0},{2,3},{3,2},{4,5},{5,4},{6,7},{7,6},{8,9},{9,8},{10,11... | collective-permute-start | bytes 1572872 | tf_op jit(solution)/shard_map/ppermute | solution.py:20
  29.8 32.3 %collective-permute-start.18 = (bf16[256,2048]{1,0:T(8,128)(2,1)S(1)}, bf16[256,2048]{1,0:T(8,128)(2,1)}, u32[]{:S(2)}, u32[]{:S(2)}) collective-permute-start(bf16[256,2048]{1,0:T(8,128)(2,1)S(1)} %copy-done), channel_id=1, source_target_pairs={{0,4},{4,0},{8,12},{12,8},{16,20},{20,16},{24,28},{28,24},{1,5},{5... | collective-permute-start | bytes 3145736 | tf_op jit(solution)/shard_map/ppermute | solution.py:20
  29.8 5.4 %collective-permute-start.7 = (bf16[256,256]{1,0:T(8,128)(2,1)S(1)}, bf16[256,256]{1,0:T(8,128)(2,1)S(1)}, u32[]{:S(2)}, u32[]{:S(2)}) collective-permute-start(bf16[256,256]{1,0:T(8,128)(2,1)S(1)} %get-tuple-element.28.refs_2_.refs_1_.refs_10_), channel_id=1, source_target_pairs={{0,4},{4,8},{8,12},{12,16},{16,20},{20,24},{24,28},{1,5},{5,9},{9,... | collective-permute-start | bytes 393224 | tf_op jit(solution)/shard_map/ppermute | solution.py:30
  32.2 4.6 %collective-permute-start.8 = (bf16[256,256]{1,0:T(8,128)(2,1)S(1)}, bf16[256,256]{1,0:T(8,128)(2,1)S(1)}, u32[]{:S(2)}, u32[]{:S(2)}) collective-permute-start(bf16[256,256]{1,0:T(8,128)(2,1)S(1)} %get-tuple-element.28.refs_2_.refs_1_.refs_10_), channel_id=1, source_target_pairs={{0,8},{4,12},{8,16},{12,20},{16,24},{20,28},{1,9},{5,13},{9,17},{1... | collective-permute-start | bytes 393224 | tf_op jit(solution)/shard_map/ppermute | solution.py:30
  42.2 12.7 %collective-permute-start.11 = (bf16[256,1024]{1,0:T(8,128)(2,1)}, bf16[256,1024]{1,0:T(8,128)(2,1)}, u32[]{:S(2)}, u32[]{:S(2)}) collective-permute-start(bf16[256,1024]{1,0:T(8,128)(2,1)} %collective-permute-done.10.refs_4_), channel_id=1, source_target_pairs={{0,4},{4,0},{8,12},{12,8},{16,20},{20,16},{24,28},{28,24},{1,5},{5... | collective-permute-start | bytes 1572872 | tf_op jit(solution)/shard_map/ppermute | solution.py:20
  42.2 12.7 %collective-permute-start.9 = (bf16[512,256]{1,0:T(8,128)(2,1)S(1)}, bf16[512,256]{1,0:T(8,128)(2,1)}, u32[]{:S(2)}, u32[]{:S(2)}) collective-permute-start(bf16[512,256]{1,0:T(8,128)(2,1)S(1)} %get-tuple-element.39.refs_1_), channel_id=1, source_target_pairs={{0,1},{1,0},{2,3},{3,2},{4,5},{5,4},{6,7},{7,6},{8,9},{9,8},{10,11... | collective-permute-start | bytes 786440 | tf_op jit(solution)/shard_map/ppermute | solution.py:20
  43.8 3.2 %collective-permute-start.12 = (bf16[256,256]{1,0:T(8,128)(2,1)S(1)}, bf16[256,256]{1,0:T(8,128)(2,1)S(1)}, u32[]{:S(2)}, u32[]{:S(2)}) collective-permute-start(bf16[256,256]{1,0:T(8,128)(2,1)S(1)} %get-tuple-element.44), channel_id=1, source_target_pairs={{4,0},{8,4},{12,8},{16,12},{20,16},{24,20},{28,24},{5,1},{9,5},{13... | collective-permute-start | bytes 393224 | tf_op jit(solution)/shard_map/ppermute | solution.py:30
  45.1 8.4 %collective-permute-start.13 = (bf16[256,256]{1,0:T(8,128)(2,1)S(1)}, bf16[256,256]{1,0:T(8,128)(2,1)S(1)}, u32[]{:S(2)}, u32[]{:S(2)}) collective-permute-start(bf16[256,256]{1,0:T(8,128)(2,1)S(1)} %get-tuple-element.45), channel_id=1, source_target_pairs={{8,0},{12,4},{16,8},{20,12},{24,16},{28,20},{9,1},{13,5},{17,9},{2... | collective-permute-start | bytes 393224 | tf_op jit(solution)/shard_map/ppermute | solution.py:30
  53.6 5.3 %collective-permute-start.14 = (bf16[256,256]{1,0:T(8,128)(2,1)S(1)}, bf16[256,256]{1,0:T(8,128)(2,1)S(1)}, u32[]{:S(2)}, u32[]{:S(2)}) collective-permute-start(bf16[256,256]{1,0:T(8,128)(2,1)S(1)} %shard_map.91.refs_2_), channel_id=1, source_target_pairs={{0,1},{1,0},{2,3},{3,2},{4,5},{5,4},{6,7},{7,6},{8,9},{9,8},{10,11... | collective-permute-start | bytes 393224 | tf_op jit(solution)/shard_map/ppermute | solution.py:20
  54.8 7.3 %collective-permute-start.16 = (bf16[512,256]{1,0:T(8,128)(2,1)S(1)}, bf16[512,256]{1,0:T(8,128)(2,1)S(1)}, u32[]{:S(2)}, u32[]{:S(2)}) collective-permute-start(bf16[512,256]{1,0:T(8,128)(2,1)S(1)} %get-tuple-element.39.refs_1_), channel_id=1, source_target_pairs={{0,4},{4,0},{8,12},{12,8},{16,20},{20,16},{24,28},{28,24},{1,5},{5... | collective-permute-start | bytes 786440 | tf_op jit(solution)/shard_map/ppermute | solution.py:20
  59.4 2.7 %collective-permute-start.17 = (bf16[256,256]{1,0:T(8,128)(2,1)S(1)}, bf16[256,256]{1,0:T(8,128)(2,1)S(1)}, u32[]{:S(2)}, u32[]{:S(2)}) collective-permute-start(bf16[256,256]{1,0:T(8,128)(2,1)S(1)} %get-tuple-element.48.refs_2_), channel_id=1, source_target_pairs={{0,4},{4,0},{8,12},{12,8},{16,20},{20,16},{24,28},{28,24},{1,5},{5... | collective-permute-start | bytes 393224 | tf_op jit(solution)/shard_map/ppermute | solution.py:20
  59.5 15.2 %collective-permute-start.15 = (bf16[256,512]{1,0:T(8,128)(2,1)S(1)}, bf16[256,512]{1,0:T(8,128)(2,1)S(1)}, u32[]{:S(2)}, u32[]{:S(2)}) collective-permute-start(bf16[256,512]{1,0:T(8,128)(2,1)S(1)} %get-tuple-element.47), channel_id=1, source_target_pairs={{0,2},{1,3},{2,0},{3,1},{4,6},{5,7},{6,4},{7,5},{8,10},{9,11},{10,... | collective-permute-start | bytes 786440 | tf_op jit(solution)/shard_map/ppermute | solution.py:25
  64.4 13.0 %collective-permute-start.19 = (bf16[96,2048]{1,0:T(8,128)(2,1)S(1)}, bf16[96,2048]{1,0:T(8,128)(2,1)S(1)}, u32[]{:S(2)}, u32[]{:S(2)}) collective-permute-start(bf16[96,2048]{1,0:T(8,128)(2,1)S(1)} %get-tuple-element.50), channel_id=1, source_target_pairs={{0,24},{4,28},{8,16},{12,20},{16,8},{20,12},{24,0},{28,4},{1,25},{... | collective-permute-start | bytes 1179656 | tf_op jit(solution)/shard_map/ppermute | solution.py:20
  65.8 20.1 %collective-permute-start.20 = (bf16[96,2048]{1,0:T(8,128)(2,1)S(1)}, bf16[96,2048]{1,0:T(8,128)(2,1)S(1)}, u32[]{:S(2)}, u32[]{:S(2)}) collective-permute-start(bf16[96,2048]{1,0:T(8,128)(2,1)S(1)} %get-tuple-element.51), channel_id=1, source_target_pairs={{0,8},{4,12},{8,0},{12,4},{16,24},{20,28},{24,16},{28,20},{1,9},{5... | collective-permute-start | bytes 1179656 | tf_op jit(solution)/shard_map/ppermute | solution.py:20
  68.3 17.6 %collective-permute-start.21 = (bf16[96,2048]{1,0:T(8,128)(2,1)S(1)}, bf16[96,2048]{1,0:T(8,128)(2,1)S(1)}, u32[]{:S(2)}, u32[]{:S(2)}) collective-permute-start(bf16[96,2048]{1,0:T(8,128)(2,1)S(1)} %get-tuple-element.52), channel_id=1, source_target_pairs={{0,16},{4,20},{8,24},{12,28},{16,0},{20,4},{24,8},{28,12},{1,17},{... | collective-permute-start | bytes 1179656 | tf_op jit(solution)/shard_map/ppermute | solution.py:20
  (2 other events, 2.0 us)
